TPU v7x, 32 devices: a whole 2x2x4 slice. The times are simulated.
32 devices in a mesh: req: 4 (over z), head: 4 (over y, x), blk: 2 (over core).
Axes of the slice: x: 2, y: 2, z: 4, core: 2. Of those that a mesh axis runs over, the one named last changes fastest.
Arguments:
- group_rows: bfloat16 [8, 256, 2048], P(None, 'req', ('head', 'blk')), may hold values from -6 to 6
- slot_request: int32 [8], replicated, may hold values from 0 to 7, each once
- cache_len: int32 [8], replicated, may hold values from 1 to 512, as said below
- group_len: int32 [8], replicated, may hold values from 1 to 256, as said below
- attn_cache: bfloat16 [2, 8, 512, 2048], P(None, 'req', None, ('head', 'blk')), as said below
- hand_cache: bfloat16 [2, 2, 8, 512, 2048], P('blk', None, None, 'req', 'head'), may hold values from -6 to 6
- query_weight: bfloat16 [2048, 2048], P(None, ('head', 'blk')), may hold values from -0.125 to 0.125
- key_weight: bfloat16 [2048, 2048], P(None, ('head', 'blk')), may hold values from -0.125 to 0.125
- value_weight: bfloat16 [2048, 2048], P(None, ('head', 'blk')), may hold values from -0.125 to 0.125
- out_weight: bfloat16 [2048, 2048], P(('head', 'blk')), may hold values from -0.125 to 0.125
- query_gain: float32 [2048], P(('head', 'blk')), may hold values from 0.5 to 1.5
- key_gain: float32 [2048], P(('head', 'blk')), may hold values from 0.5 to 1.5
- attn_gain: float32 [2048], replicated, may hold values from 0.1 to 1.9
- mlp_gain: float32 [2048], replicated, may hold values from 0.1 to 1.9
- gate_weight: bfloat16 [2048, 4096], P(None, ('head', 'blk')), may hold values from -0.125 to 0.125
- up_weight: bfloat16 [2048, 4096], P(None, ('head', 'blk')), may hold values from -0.125 to 0.125
- down_weight: bfloat16 [4096, 2048], P(('head', 'blk')), may hold values from -0.09375 to 0.09375
Outputs:
- layer_out: bfloat16 [8, 256, 2048], P(None, 'req', ('head', 'blk'))
- relaid: bfloat16 [2, 2, 8, 512, 2048], P('blk', None, 'req', None, 'head')
Inputs may be any that keep to these rules, and one draw needn't show every extreme that they name: `cache_len`: some request has exactly 512 cached tokens. `group_len`: some request has exactly 256 valid new tokens. `attn_cache`: entry s along the request dimension belongs to request slot_request[s]; positions from cache_len of that request on are not read.
All inputs are finite; a program needn't handle non-finite values.
Results may differ from a plain program's by a relative error of at most 0.009.
The roundings to bfloat16 on the way count: a program that leaves them out, or rounds other values in their place, can miss the bound.
Values may be sent and summed in bfloat16 or wider, within the bound.
A program may use at most 128 MiB of HBM per device.

v0:
```python
import jax
import jax.numpy as jnp
from jax import lax
from jax.sharding import PartitionSpec as P

HD = 128
EPSILON = 1e-06
ROPE_BASE = 500000.0


def rotate(values, places):
    half_dim = values.shape[-1] // 2
    frequency = ROPE_BASE ** (-(jnp.arange(half_dim, dtype=jnp.float32) * 2.0 / values.shape[-1]))
    angles = places[..., None].astype(jnp.float32) * frequency
    cosine_part = jnp.cos(angles)[..., None, :]
    sine_part = jnp.sin(angles)[..., None, :]
    first_half = values[..., :half_dim]
    second_half = values[..., half_dim:]
    return jnp.concatenate(
        [
            first_half * cosine_part - second_half * sine_part,
            second_half * cosine_part + first_half * sine_part,
        ],
        axis=-1,
    )


def send_home(blocks, inverse):
    received = lax.all_to_all(blocks, "req", split_axis=1, concat_axis=0, tiled=True)
    return jnp.take(received, inverse, axis=0)


def on_device(
    group_rows,
    slot_request,
    cache_len,
    group_len,
    attn_cache,
    hand_cache,
    query_weight,
    key_weight,
    value_weight,
    out_weight,
    query_gain,
    key_gain,
    attn_gain,
    mlp_gain,
    gate_weight,
    up_weight,
    down_weight,
):
    slot_total = slot_request.shape[0]
    slot_count = slot_total // lax.axis_size("req")
    first_slot = lax.axis_index("req") * slot_count
    own_requests = lax.dynamic_slice_in_dim(slot_request, first_slot, slot_count)
    cached = jnp.take(cache_len, own_requests)
    group_valid = jnp.take(group_len, own_requests)
    inverse = (
        jnp.zeros_like(slot_request).at[slot_request].set(jnp.arange(slot_total, dtype=jnp.int32))
    )
    reordered = jnp.take(hand_cache, slot_request, axis=2)
    relaid = lax.all_to_all(reordered, "req", split_axis=2, concat_axis=3, tiled=True)
    local_x = lax.all_to_all(
        jnp.take(group_rows, slot_request, axis=0), "req", split_axis=0, concat_axis=1, tiled=True
    )
    tokens = local_x.shape[1]
    row_width = local_x.shape[2]
    model_width = row_width * lax.axis_size(("head", "blk"))
    feature_start = lax.axis_index(("head", "blk")) * row_width
    full_x = lax.all_gather(local_x, ("head", "blk"), axis=2, tiled=True)
    rows_x = full_x.reshape(-1, model_width)
    queries = jnp.dot(rows_x, query_weight, preferred_element_type=jnp.float32)
    keys_new = jnp.dot(rows_x, key_weight, preferred_element_type=jnp.float32)
    values_new = jnp.dot(rows_x, value_weight, preferred_element_type=jnp.float32)
    square_sums = lax.psum(
        (jnp.sum(queries * queries, axis=-1), jnp.sum(keys_new * keys_new, axis=-1)),
        ("head", "blk"),
    )
    queries = queries * lax.rsqrt(square_sums[0] / model_width + EPSILON)[:, None] * query_gain
    keys_new = keys_new * lax.rsqrt(square_sums[1] / model_width + EPSILON)[:, None] * key_gain
    heads_here = row_width // HD
    places = cached[:, None] + jnp.arange(tokens, dtype=jnp.int32)[None, :]
    queries = rotate(queries.reshape(slot_count, tokens, heads_here, HD), places).astype(
        jnp.bfloat16
    )
    keys_new = rotate(keys_new.reshape(slot_count, tokens, heads_here, HD), places).astype(
        jnp.bfloat16
    )
    values_new = values_new.astype(jnp.bfloat16).reshape(slot_count, tokens, heads_here, HD)
    keys_old = attn_cache[0].reshape(slot_count, -1, heads_here, HD)
    values_old = attn_cache[1].reshape(slot_count, -1, heads_here, HD)
    score_scale = 1.0 / HD**0.5
    span_old = keys_old.shape[1]
    old_scores = (
        jnp.einsum("sthd,sjhd->shtj", queries, keys_old, preferred_element_type=jnp.float32)
        * score_scale
    )
    new_scores = (
        jnp.einsum("sthd,sjhd->shtj", queries, keys_new, preferred_element_type=jnp.float32)
        * score_scale
    )
    old_mask = (jnp.arange(span_old)[None, :] < cached[:, None])[:, None, None, :]
    columns = jnp.arange(tokens)
    new_mask = (columns[None, None, :] <= columns[None, :, None]) & (
        columns[None, None, :] < group_valid[:, None, None]
    )
    new_mask = new_mask[:, None, :, :]
    scores = jnp.concatenate(
        [jnp.where(old_mask, old_scores, -1e30), jnp.where(new_mask, new_scores, -1e30)], axis=-1
    )
    row_top = jnp.max(scores, axis=-1, keepdims=True)
    weights = jnp.exp(scores - row_top)
    weights = (weights / jnp.sum(weights, axis=-1, keepdims=True)).astype(jnp.bfloat16)
    stacked = jnp.concatenate([values_old, values_new], axis=1)
    attended = jnp.einsum("shtj,sjhd->sthd", weights, stacked, preferred_element_type=jnp.float32)
    attended = attended.astype(jnp.bfloat16).reshape(-1, row_width)
    partial_value = jnp.dot(attended, out_weight, preferred_element_type=jnp.float32)
    totals = lax.psum(partial_value, ("head", "blk"))
    normed = (
        totals * lax.rsqrt(jnp.mean(totals * totals, axis=-1, keepdims=True) + EPSILON) * attn_gain
    )
    state_full = (rows_x.astype(jnp.float32) + normed).astype(jnp.bfloat16)
    state_part = lax.dynamic_slice_in_dim(state_full, feature_start, row_width, 1)
    gate_act = jnp.dot(state_full, gate_weight, preferred_element_type=jnp.float32)
    up_act = jnp.dot(state_full, up_weight, preferred_element_type=jnp.float32)
    inner = (jax.nn.silu(gate_act) * up_act).astype(jnp.bfloat16)
    down_sum = jnp.dot(inner, down_weight, preferred_element_type=jnp.float32)
    down_share = lax.psum_scatter(down_sum, ("head", "blk"), scatter_dimension=1, tiled=True)
    down_power = lax.psum(jnp.sum(down_share * down_share, axis=-1), ("head", "blk"))
    mgain_part = lax.dynamic_slice_in_dim(mlp_gain, feature_start, row_width)
    result = (
        state_part.astype(jnp.float32)
        + down_share * lax.rsqrt(down_power / model_width + EPSILON)[:, None] * mgain_part
    ).astype(jnp.bfloat16)
    layer_out = send_home(result.reshape(slot_count, tokens, row_width), inverse)
    return (layer_out, relaid)


def solution(mesh):
    in_specs = (
        P(None, "req", ("head", "blk")),
        P(),
        P(),
        P(),
        P(None, "req", None, ("head", "blk")),
        P("blk", None, None, "req", "head"),
        P(None, ("head", "blk")),
        P(None, ("head", "blk")),
        P(None, ("head", "blk")),
        P(("head", "blk"), None),
        P(("head", "blk")),
        P(("head", "blk")),
        P(),
        P(),
        P(None, ("head", "blk")),
        P(None, ("head", "blk")),
        P(("head", "blk"), None),
    )
    out_specs = (P(None, "req", ("head", "blk")), P("blk", None, "req", None, "head"))
    return jax.shard_map(
        on_device, mesh=mesh, in_specs=in_specs, out_specs=out_specs, check_vma=False
    )
```

profile of v0, /device:TPU:0, one launch (start us, length us, event | category | flops | bytes accessed | tf_op | source)
XLA Modules:
  0.0 288.7 jit_solution(8035457051612961432)
XLA Ops:
  7.3 0.8 compare_select_fusion.2
  8.1 0.7 compare_and_fusion.2
  8.7 1.5 gather_fusion.1
  10.2 0.1 broadcast_select_fusion.1
  10.3 15.0 %all_to_all.54 = bf16[8,64,256]{2,1,0:T(8,128)(2,1)S(1)} all-to-all(bf16[8,64,256]{2,1,0:T(8,128)(2,1)S(1)} %broadcast_select_fusion.1), channel_id=1, replica_groups=mesh['req'=4,'head'=4,'blk'=2] {'req'}, dimensions={0} | all-to-all | bytes 524288 | tf_op jit(solution)/shard_map/all_to_all | solution.py:63
  25.3 0.7 copy.53
  26.1 0.1 compare_select_fusion.1
  26.2 0.6 gather_fusion.2
  26.9 0.6 gather_fusion.3
  27.5 1.3 fusion.25
  28.8 1.0 copy.76
  29.8 1.0 copy.54
  30.9 0.1 broadcast_select_fusion.3
  30.9 0.1 iota_compare_fusion.2
  31.0 0.1 add_convert_fusion.4
  31.1 0.1 iota_compare_fusion.1
  31.2 1.7 multiply_cosine_fusion
  33.0 20.6 %all-gather.2.cloned.1.call-done = bf16[2,256,2048]{2,1,0:T(8,128)(2,1)} async-done(((bf16[2,256,256]{2,1,0:T(8,128)(2,1)}), bf16[2,256,2048]{2,1,0:T(8,128)(2,1)}) %all-gather.2.cloned.1.call-update) | async-done | bytes 2097168 | tf_op jit(solution)/shard_map/all_gather | solution.py:70
  53.6 2.8 multiply_reduce_fusion.2
  56.3 2.8 multiply_reduce_fusion.3
  59.1 13.1 %all-reduce = (f32[512]{0:T(512)S(1)}, f32[512]{0:T(512)S(1)}) all-reduce(f32[512]{0:T(512)S(1)} %get-tuple-element.22, f32[512]{0:T(512)S(1)} %get-tuple-element.24), channel_id=1, replica_groups=mesh['req'=4,'head'=4,'blk'=2] {'head','blk'}, use_global_device_ids=true, to_apply=%region_3.6 | all-reduce | flops 1024 | bytes 8192 | tf_op jit(solution)/shard_map/psum | solution.py:75
  72.2 0.8 multiply_multiply_fusion
  73.0 0.3 reshape.220
  73.4 1.0 fusion.27
  74.3 1.1 copy.77
  75.5 1.1 copy.78
  76.7 1.9 multiply_multiply_fusion.1
  78.6 2.2 reshape.152
  80.8 2.0 fusion.26
  82.8 2.0 copy.74
  84.7 1.9 copy.75
  86.7 3.3 %convolution_convert_fusion = bf16[512,256]{1,0:T(8,128)(2,1)} fusion(bf16[512,2048]{1,0:T(8,128)(2,1)} %bitcast.50, bf16[2048,256]{1,0:T(8,128)(2,1)} %param.29), kind=kOutput, calls=%fused_computation.20 | convolution fusion | flops 537001984 | bytes 3407872 | tf_op jit(solution)/shard_map/dot_general | solution.py:74
  90.0 1.7 reshape.151
  91.7 1.8 copy.55
  93.5 1.6 subtract_convert_fusion.1
  95.1 0.6 fusion.28
  95.7 0.6 fusion.29
  96.3 1.0 fusion.1
  97.4 2.0 fusion.6
  99.4 1.1 copy.64
  100.5 2.7 fusion.12
  103.2 0.2 reduce-scatter.2.cloned.1.call-start
  103.5 81.0 %all-reduce.3.cloned.1.call-done = f32[512,2048]{1,0:T(8,128)} async-done(((f32[512,2048]{1,0:T(8,128)}), f32[512,2048]{1,0:T(8,128)}) %all-reduce.3.cloned.1.call-update) | async-done | bytes 4194320 | tf_op jit(solution)/shard_map/psum | solution.py:118
  184.4 2.7 multiply_reduce_fusion
  187.1 0.7 copy-done.3
  187.9 2.5 add_convert_fusion
  190.4 1.3 copy-done.4
  191.7 1.3 fusion.30
  192.9 7.2 %fusion.7 = f32[512,2048]{1,0:T(8,128)} fusion(bf16[512,2048]{1,0:T(8,128)(2,1)} %param.37, bf16[512,2048]{1,0:T(8,128)(2,1)} %copy-done.4, bf16[2048,512]{1,0:T(8,128)(2,1)} %param.36, f32[512,512]{1,0:T(8,128)S(1)} %fusion.30), kind=kOutput, calls=%fused_computation.22 | convolution fusion | flops 2149056512 | bytes 11534336 | tf_op jit(solution)/shard_map/dot_general | solution.py:127
  200.2 2.0 gather_fusion
  202.2 3.2 %bitcast_select_fusion = bf16[1,2,8,128,512]{4,3,1,0,2:T(8,128)(2,1)} fusion(bf16[8,2,128,512]{3,2,1,0:T(8,128)(2,1)} %gather_fusion, pred[8]{0:T(512)(128)(4,1)S(1)} %compare_and_fusion.2), kind=kLoop, calls=%fused_computation.12 | loop fusion | flops 1048576 | bytes 4194312 | tf_op jit(solution)/shard_map/jit(_take)/select_n | solution.py:61
  205.4 4.6 %all-to-all-start.2 = ((bf16[1,2,8,128,512]{4,3,1,0,2:T(8,128)(2,1)}), bf16[1,2,8,128,512]{4,3,1,0,2:T(8,128)(2,1)}, u32[]{:S(2)}, u32[]{:S(2)}) async-start(bf16[1,2,8,128,512]{4,3,1,0,2:T(8,128)(2,1)} %bitcast_select_fusion), calls=%async_computation.3 | async-start | bytes 4194304 | tf_op jit(solution)/shard_map/all_to_all | solution.py:62
  210.0 0.7 scatter_custom_fusion
  210.8 0.8 dynamic_slice.11
  211.5 40.2 %reduce-scatter.2.cloned.1.call-done = f32[512,256]{1,0:T(8,128)} async-done(((f32[512,2048]{1,0:T(8,128)}), f32[512,256]{1,0:T(8,128)}) %reduce-scatter.2.cloned.1.call-update) | async-done | bytes 524304 | tf_op jit(solution)/shard_map/reduce_scatter | solution.py:128
  251.8 1.2 multiply_reduce_fusion.1
  253.0 13.1 %psum.31 = f32[512]{0:T(512)S(1)} all-reduce(f32[512]{0:T(512)S(1)} %multiply_reduce_fusion.1), channel_id=1, replica_groups=mesh['req'=4,'head'=4,'blk'=2] {'head','blk'}, use_global_device_ids=true, to_apply=%region_11.14 | all-reduce | flops 512 | bytes 4096 | tf_op jit(solution)/shard_map/psum | solution.py:129
  266.1 1.3 add_convert_fusion.1
  267.3 1.0 copy.65
  268.3 4.2 %all-to-all-start.1 = ((bf16[2,256,256]{2,0,1:T(2,128)(2,1)}), bf16[2,256,256]{2,0,1:T(2,128)(2,1)S(1)}, u32[]{:S(2)}, u32[]{:S(2)}) async-start(bf16[2,256,256]{2,0,1:T(2,128)(2,1)} %copy.65), calls=%async_computation.2 | async-start | bytes 524288 | tf_op jit(solution)/shard_map/all_to_all | solution.py:29
  272.5 3.1 %copy.68 = bf16[1,2,2,4,128,512]{5,4,3,2,1,0:T(8,128)(2,1)} copy(bf16[1,2,2,4,128,512]{5,4,1,2,3,0:T(8,128)(2,1)} %bitcast.15) | data formatting | bytes 4194304 | tf_op jit(solution)/shard_map/all_to_all | solution.py:62
  275.6 5.1 %all-to-all-done.1 = bf16[2,256,256]{2,0,1:T(2,128)(2,1)S(1)} async-done(((bf16[2,256,256]{2,0,1:T(2,128)(2,1)}), bf16[2,256,256]{2,0,1:T(2,128)(2,1)S(1)}, u32[]{:S(2)}, u32[]{:S(2)}) %all-to-all-start.1) | async-done | bytes 262176 | tf_op jit(solution)/shard_map/all_to_all | solution.py:29
  280.8 0.6 gather_fusion.4
  281.3 0.8 broadcast_select_fusion
  (47 shorter events, 0.5 us)
Async XLA Ops:
  7.2 193.0 %copy-start = (bf16[1,2,8,128,512]{4,3,2,1,0:T(8,128)(2,1)S(1)}, bf16[1,2,8,128,512]{4,3,2,1,0:T(8,128)(2,1)}, u32[]{:S(2)}) copy-start(bf16[1,2,8,128,512]{4,3,2,1,0:T(8,128)(2,1)} %param.26) | copy-start | bytes 6291460
  7.2 19.0 %copy-start.12 = (s32[8]{0:T(128)S(1)}, s32[8]{0:T(128)}, u32[]{:S(2)}) copy-start(s32[8]{0:T(128)} %param.22) | copy-start | bytes 100
  7.2 19.0 %copy-start.1 = (s32[8]{0:T(128)S(1)}, s32[8]{0:T(128)}, u32[]{:S(2)}) copy-start(s32[8]{0:T(128)} %param.23) | copy-start | bytes 100
  7.2 19.7 %copy-start.2 = (s32[8]{0:T(128)S(1)}, s32[8]{0:T(128)}, u32[]{:S(2)}) copy-start(s32[8]{0:T(128)} %param.24) | copy-start | bytes 100
  7.2 46.3 %all-gather.2.cloned.1.call-start = ((), (), s32[]{:S(2)}) async-start(), calls=%async_computation.4 | async-start | bytes 2359296 | tf_op jit(solution)/shard_map/all_gather | solution.py:70
  8.1 0.7 copy-start.11
  26.1 158.3 %all-reduce.3.cloned.1.call-start = ((), (), s32[]{:S(2)}) async-start(), calls=%async_computation.5 | async-start | bytes 8388608 | tf_op jit(solution)/shard_map/psum | solution.py:118
  53.6 2.8 copy-start.6
  93.5 1.6 copy-start.5
  96.2 1.0 copy-start.8
  96.2 1.1 copy-start.9
  97.4 3.2 %copy-start.7 = (bf16[256,2048]{1,0:T(8,128)(2,1)S(1)}, bf16[256,2048]{1,0:T(8,128)(2,1)}, u32[]{:S(2)}) copy-start(bf16[256,2048]{1,0:T(8,128)(2,1)} %param.30) | copy-start | bytes 3145732
  103.2 83.9 %copy-start.10 = (f32[2048]{0:T(1024)S(1)}, f32[2048]{0:T(1024)}, u32[]{:S(2)}) copy-start(f32[2048]{0:T(1024)} %param.33) | copy-start | bytes 24580
  103.2 148.5 %reduce-scatter.2.cloned.1.call-start = ((), (), s32[]{:S(2)}) async-start(), calls=%async_computation.6 | async-start | bytes 4718592 | tf_op jit(solution)/shard_map/reduce_scatter | solution.py:128
  184.4 3.4 %copy-start.3 = (f32[512,2048]{1,0:T(8,128)S(1)}, f32[512,2048]{1,0:T(8,128)}, u32[]{:S(2)}) copy-start(f32[512,2048]{1,0:T(8,128)} %all-reduce.3.cloned.1.call-done) | copy-start | bytes 12582916
  187.9 3.8 %copy-start.13 = (bf16[2048,512]{1,0:T(8,128)(2,1)S(1)}, bf16[2048,512]{1,0:T(8,128)(2,1)}, u32[]{:S(2)}) copy-start(bf16[2048,512]{1,0:T(8,128)(2,1)} %param.35) | copy-start | bytes 6291460
  190.3 1.3 copy-start.4
  205.4 62.9 %all-to-all-start.2 = ((bf16[1,2,8,128,512]{4,3,1,0,2:T(8,128)(2,1)}), bf16[1,2,8,128,512]{4,3,1,0,2:T(8,128)(2,1)}, u32[]{:S(2)}, u32[]{:S(2)}) async-start(bf16[1,2,8,128,512]{4,3,1,0,2:T(8,128)(2,1)} %bitcast_select_fusion), calls=%async_computation.3 | async-start | bytes 4194304 | tf_op jit(solution)/shard_map/all_to_all | solution.py:62
  268.3 12.4 %all-to-all-start.1 = ((bf16[2,256,256]{2,0,1:T(2,128)(2,1)}), bf16[2,256,256]{2,0,1:T(2,128)(2,1)S(1)}, u32[]{:S(2)}, u32[]{:S(2)}) async-start(bf16[2,256,256]{2,0,1:T(2,128)(2,1)} %copy.65), calls=%async_computation.2 | async-start | bytes 524288 | tf_op jit(solution)/shard_map/all_to_all | solution.py:29
Sparse Core Ops, SparseCore 0:
  26.2 27.3 all-gather.1
  103.3 81.0 all-reduce.2
  200.3 51.3 reduce-scatter.1
where the time goes:
time: 290 us; the launch traced here: 289 us
  waiting for transfers between devices  147 us (51%)
  blocking collectives  41.2 us (14%)
  local copies, waits for them, and re-layouts  33.5 us (12%)
  matrix products  23.2 us (8%)
  other arithmetic  20.8 us (7%)
  between operations  14 us (5%)
  starting transfers between devices  9.1 us (3%)
    psum x1, waiting for transfers between devices, on_device(): totals = lax.psum(partial_value, ('head', 'blk'))  81 us
    reduce_scatter x1, waiting for transfers between devices, on_device(): lax.psum_scatter(down_sum, ('head', 'blk'), scatter_dimension=1, tiled=True)  40.2 us
    all_gather x1, waiting for transfers between devices, on_device(): full_x = lax.all_gather(local_x, ('head', 'blk'), axis=2, tiled=True)  20.6 us
    all_to_all x1, blocking collectives, on_device(): lax.all_to_all(jnp.take(group_rows, slot_request, axis=0), 'req', split_a...  15 us
    psum x1, blocking collectives, on_device(): lax.psum(jnp.sum(down_share * down_share, axis=-1), ('head', 'blk'))  13.1 us
    psum x1, blocking collectives, on_device(): lax.psum((jnp.sum(queries * queries, axis=-1), jnp.sum(keys_new * keys_ne...  13.1 us
    unnamed x33, local copies, waits for them, and re-layouts  9.4 us
    dot_general x1, matrix products, on_device(): down_sum = jnp.dot(inner, down_weight, preferred_element_type=jnp.float32)  7.24 us
  transfers between devices with their start and end apart: 5, of which 4 were waited for; matrix products, arithmetic and copies ran while one was open for 7% of the time, Pallas kernels for 0%

commit v1 on v0

--- a/solution.py
+++ b/solution.py
@@ -67,7 +67,15 @@
     row_width = local_x.shape[2]
     model_width = row_width * lax.axis_size(("head", "blk"))
     feature_start = lax.axis_index(("head", "blk")) * row_width
-    full_x = lax.all_gather(local_x, ("head", "blk"), axis=2, tiled=True)
+    ways, here = (lax.axis_size(("head", "blk")), lax.axis_index(("head", "blk")))
+    grown, reach = (local_x, 1)
+    while reach < ways:
+        theirs = lax.ppermute(grown, ("head", "blk"), [(d, d ^ reach) for d in range(ways)])
+        mine_first = jnp.concatenate([grown, theirs], axis=2)
+        theirs_first = jnp.concatenate([theirs, grown], axis=2)
+        grown = jnp.where(here & reach == 0, mine_first, theirs_first)
+        reach = 2 * reach
+    full_x = grown
     rows_x = full_x.reshape(-1, model_width)
     queries = jnp.dot(rows_x, query_weight, preferred_element_type=jnp.float32)
     keys_new = jnp.dot(rows_x, key_weight, preferred_element_type=jnp.float32)

time: 290 us -> 313 us (1.079)
  waiting for transfers between devices: 147 us -> 163 us
  blocking collectives: 41.2 us -> 26.4 us
  starting transfers between devices: 9.1 us -> 18.5 us
  other arithmetic: 20.8 us -> 27.8 us
  local copies, waits for them, and re-layouts: 33.5 us -> 39 us
    ppermute x0 -> x3, waiting for transfers between devices: none -> 32.5 us  [on_device(): lax.ppermute(grown, ('head', 'blk'), [(d, d ^ reach) for d in range(ways)])]
    all_gather x1 -> x0, waiting for transfers between devices: 20.6 us -> none  [on_device(): full_x = lax.all_gather(local_x, ('head', 'blk'), axis=2, tiled=True)]
    all_to_all x1 -> x0, blocking collectives: 15 us -> none  [on_device(): lax.all_to_all(jnp.take(group_rows, slot_request, axis=0), 'req', split_a...]
    all_to_all x0 -> x1, waiting for transfers between devices: none -> 6.9 us  [on_device(): lax.all_to_all(jnp.take(group_rows, slot_request, axis=0), 'req', split_a...]
    all_to_all x0 -> x1, starting transfers between devices: none -> 6.32 us  [on_device(): lax.all_to_all(jnp.take(group_rows, slot_request, axis=0), 'req', split_a...]
    ppermute x0 -> x3, starting transfers between devices: none -> 3.21 us  [on_device(): lax.ppermute(grown, ('head', 'blk'), [(d, d ^ reach) for d in range(ways)])]
    unnamed x33 -> x37, local copies, waits for them, and re-layouts: 9.4 us -> 11.7 us
  transfers between devices with their start and end apart: 5 -> 8, of which waited for: 4 -> 6; matrix products, arithmetic and copies ran while one was open for 7% -> 7% of each run, Pallas kernels for 0% -> 0%
where the time goes in v1:
time: 313 us; the launch traced here: 312 us
  waiting for transfers between devices  163 us (52%)
  local copies, waits for them, and re-layouts  39 us (12%)
  other arithmetic  27.8 us (9%)
  blocking collectives  26.4 us (8%)
  matrix products  22.8 us (7%)
  starting transfers between devices  18.5 us (6%)
  between operations  14.3 us (5%)
    psum x1, waiting for transfers between devices, on_device(): totals = lax.psum(partial_value, ('head', 'blk'))  78.3 us
    reduce_scatter x1, waiting for transfers between devices, on_device(): lax.psum_scatter(down_sum, ('head', 'blk'), scatter_dimension=1, tiled=True)  40.2 us
    ppermute x3, waiting for transfers between devices, on_device(): lax.ppermute(grown, ('head', 'blk'), [(d, d ^ reach) for d in range(ways)])  32.5 us
    psum x1, blocking collectives, on_device(): lax.psum((jnp.sum(queries * queries, axis=-1), jnp.sum(keys_new * keys_ne...  13.3 us
    psum x1, blocking collectives, on_device(): lax.psum(jnp.sum(down_share * down_share, axis=-1), ('head', 'blk'))  13.1 us
    unnamed x37, local copies, waits for them, and re-layouts  11.7 us
    dot_general x1, matrix products, on_device(): down_sum = jnp.dot(inner, down_weight, preferred_element_type=jnp.float32)  7.24 us
    all_to_all x1, waiting for transfers between devices, on_device(): lax.all_to_all(jnp.take(group_rows, slot_request, axis=0), 'req', split_a...  6.9 us
  transfers between devices with their start and end apart: 8, of which 6 were waited for; matrix products, arithmetic and copies ran while one was open for 7% of the time, Pallas kernels for 0%

profile of v1, /device:TPU:0, one launch (start us, length us, event | category | flops | bytes accessed | tf_op | source)
XLA Modules:
  0.0 311.8 jit_solution(9282600704694906613)
XLA Ops:
  7.2 0.8 compare_select_fusion.2
  8.0 0.7 compare_and_fusion.2
  8.7 1.5 gather_fusion.1
  10.2 0.8 broadcast_select_fusion.1
  11.0 6.3 %all-to-all-start = ((bf16[8,64,256]{2,1,0:T(8,128)(2,1)}), bf16[8,64,256]{2,1,0:T(8,128)(2,1)S(1)}, u32[]{:S(2)}, u32[]{:S(2)}) async-start(bf16[8,64,256]{2,1,0:T(8,128)(2,1)} %broadcast_select_fusion.1), calls=%async_computation | async-start | bytes 524288 | tf_op jit(solution)/shard_map/all_to_all | solution.py:63
  17.3 0.7 compare_select_fusion.1
  18.1 1.3 fusion.28
  19.3 6.9 %all-to-all-done = bf16[8,64,256]{2,1,0:T(8,128)(2,1)S(1)} async-done(((bf16[8,64,256]{2,1,0:T(8,128)(2,1)}), bf16[8,64,256]{2,1,0:T(8,128)(2,1)S(1)}, u32[]{:S(2)}, u32[]{:S(2)}) %all-to-all-start) | async-done | bytes 262176 | tf_op jit(solution)/shard_map/all_to_all | solution.py:63
  26.2 0.7 copy-done.6
  26.9 1.0 copy.53
  28.0 0.6 gather_fusion.2
  28.7 0.6 gather_fusion.3
  29.3 1.0 copy.76
  30.3 1.0 copy.54
  31.4 1.2 maximum_select_fusion.4
  32.6 1.6 collective-permute-start.1
  34.3 12.6 %collective-permute-done.1 = bf16[2,256,512]{2,1,0:T(8,128)(2,1)S(1)} collective-permute-done((bf16[2,256,512]{2,1,0:T(8,128)(2,1)S(1)}, bf16[2,256,512]{2,1,0:T(8,128)(2,1)S(1)}, u32[]{:S(2)}, u32[]{:S(2)}) %collective-permute-start.1) | collective-permute-done | bytes 524320 | tf_op jit(solution)/shard_map/ppermute | solution.py:73
  47.3 1.6 collective-permute-start.2
  49.0 1.8 multiply_cosine_fusion
  50.8 1.2 maximum_select_fusion.3
  52.3 19.8 %collective-permute-done.2 = bf16[2,256,1024]{2,1,0:T(8,128)(2,1)S(1)} collective-permute-done((bf16[2,256,1024]{2,1,0:T(8,128)(2,1)S(1)}, bf16[2,256,1024]{2,1,0:T(8,128)(2,1)S(1)}, u32[]{:S(2)}, u32[]{:S(2)}) %collective-permute-start.2) | collective-permute-done | bytes 1048608 | tf_op jit(solution)/shard_map/ppermute | solution.py:73
  72.1 1.7 multiply_reduce_fusion.2
  73.8 2.2 multiply_reduce_fusion.3
  76.0 13.3 %all-reduce = (f32[512]{0:T(512)}, f32[512]{0:T(512)}) all-reduce(f32[512]{0:T(512)S(1)} %get-tuple-element.22, f32[512]{0:T(512)} %get-tuple-element.24), channel_id=1, replica_groups=mesh['req'=4,'head'=4,'blk'=2] {'head','blk'}, use_global_device_ids=true, to_apply=%region_3.6 | all-reduce | flops 1024 | bytes 8192 | tf_op jit(solution)/shard_map/psum | solution.py:83
  89.3 0.7 add_rsqrt_fusion.2
  90.0 2.0 multiply_multiply_fusion
  92.0 2.2 reshape.231
  94.2 2.0 fusion.30
  96.2 2.0 copy.77
  98.1 1.9 copy.78
  100.1 2.0 multiply_multiply_fusion.1
  102.0 2.2 reshape.163
  104.2 2.0 fusion.29
  106.2 2.0 copy.74
  108.2 2.0 copy.75
  110.1 3.3 %convolution_convert_fusion = bf16[512,256]{1,0:T(8,128)(2,1)} fusion(bf16[2048,256]{1,0:T(8,128)(2,1)} %param.29, bf16[512,1024]{1,0:T(8,128)(2,1)} %bitcast.60, bf16[512,1024]{1,0:T(8,128)(2,1)S(1)} %maximum_select_fusion.1, pred[]{:T(512)S(6)} %eq.9), kind=kOutput, calls=%fused_computation.19 | convolution fusion | flops 546439168 | bytes 3407873 | tf_op jit(solution)/shard_map/dot_general | solution.py:82
  113.4 1.7 reshape.162
  115.1 1.8 copy.55
  116.9 1.9 subtract_convert_fusion.1
  120.1 1.0 fusion.1
  121.1 2.0 fusion.5
  123.2 1.1 copy.64
  124.3 3.9 %fusion.13 = f32[512,2048]{1,0:T(8,128)} fusion(bf16[256,2048]{1,0:T(8,128)(2,1)} %param.30, bf16[64,8,2,128]{3,2,1,0:T(2,128)(2,1)S(1)} %bitcast.53), kind=kOutput, calls=%fused_computation.44 | convolution fusion | flops 536870912 | bytes 5505024 | tf_op jit(solution)/shard_map/dot_general | solution.py:125
  128.5 78.3 %all-reduce.3.cloned.1.call-done = f32[512,2048]{1,0:T(8,128)} async-done(((f32[512,2048]{1,0:T(8,128)}), f32[512,2048]{1,0:T(8,128)}) %all-reduce.3.cloned.1.call-update) | async-done | bytes 4194320 | tf_op jit(solution)/shard_map/psum | solution.py:126
  206.8 2.7 multiply_reduce_fusion
  209.5 0.7 copy-done.3
  210.2 3.0 add_convert_fusion
  213.2 1.3 copy-done.4
  214.5 1.3 fusion.33
  215.8 7.2 %fusion.9 = f32[512,2048]{1,0:T(8,128)} fusion(bf16[512,2048]{1,0:T(8,128)(2,1)} %param.37, f32[512,512]{1,0:T(8,128)S(1)} %fusion.33, bf16[512,2048]{1,0:T(8,128)(2,1)} %copy-done.4, bf16[2048,512]{1,0:T(8,128)(2,1)} %param.36), kind=kOutput, calls=%fused_computation.27 | convolution fusion | flops 2149056512 | bytes 11534336 | tf_op jit(solution)/shard_map/dot_general | solution.py:135
  223.1 2.0 gather_fusion
  225.1 3.2 %bitcast_select_fusion = bf16[1,2,8,128,512]{4,3,1,0,2:T(8,128)(2,1)} fusion(bf16[8,2,128,512]{3,2,1,0:T(8,128)(2,1)} %gather_fusion, pred[8]{0:T(512)(128)(4,1)S(1)} %compare_and_fusion.2), kind=kLoop, calls=%fused_computation.13 | loop fusion | flops 1048576 | bytes 4194312 | tf_op jit(solution)/shard_map/jit(_take)/select_n | solution.py:61
  228.3 4.6 %all-to-all-start.2 = ((bf16[1,2,8,128,512]{4,3,1,0,2:T(8,128)(2,1)}), bf16[1,2,8,128,512]{4,3,1,0,2:T(8,128)(2,1)}, u32[]{:S(2)}, u32[]{:S(2)}) async-start(bf16[1,2,8,128,512]{4,3,1,0,2:T(8,128)(2,1)} %bitcast_select_fusion), calls=%async_computation.3 | async-start | bytes 4194304 | tf_op jit(solution)/shard_map/all_to_all | solution.py:62
  232.9 0.7 scatter_custom_fusion
  233.6 0.8 dynamic_slice.11
  234.4 40.2 %reduce-scatter.2.cloned.1.call-done = f32[512,256]{1,0:T(8,128)} async-done(((f32[512,2048]{1,0:T(8,128)}), f32[512,256]{1,0:T(8,128)}) %reduce-scatter.2.cloned.1.call-update) | async-done | bytes 524304 | tf_op jit(solution)/shard_map/reduce_scatter | solution.py:136
  274.6 1.2 multiply_reduce_fusion.1
  275.8 13.1 %psum.31 = f32[512]{0:T(512)S(1)} all-reduce(f32[512]{0:T(512)S(1)} %multiply_reduce_fusion.1), channel_id=1, replica_groups=mesh['req'=4,'head'=4,'blk'=2] {'head','blk'}, use_global_device_ids=true, to_apply=%region_11.14 | all-reduce | flops 512 | bytes 4096 | tf_op jit(solution)/shard_map/psum | solution.py:137
  288.9 1.3 add_convert_fusion.1
  290.1 1.0 copy.65
  291.1 4.2 %all-to-all-start.1 = ((bf16[2,256,256]{2,0,1:T(2,128)(2,1)}), bf16[2,256,256]{2,0,1:T(2,128)(2,1)S(1)}, u32[]{:S(2)}, u32[]{:S(2)}) async-start(bf16[2,256,256]{2,0,1:T(2,128)(2,1)} %copy.65), calls=%async_computation.2 | async-start | bytes 524288 | tf_op jit(solution)/shard_map/all_to_all | solution.py:29
  295.3 3.1 copy.68
  298.4 5.1 %all-to-all-done.1 = bf16[2,256,256]{2,0,1:T(2,128)(2,1)S(1)} async-done(((bf16[2,256,256]{2,0,1:T(2,128)(2,1)}), bf16[2,256,256]{2,0,1:T(2,128)(2,1)S(1)}, u32[]{:S(2)}, u32[]{:S(2)}) %all-to-all-start.1) | async-done | bytes 262176 | tf_op jit(solution)/shard_map/all_to_all | solution.py:29
  304.1 0.8 broadcast_select_fusion
  (59 shorter events, 3.3 us)
Async XLA Ops:
  7.2 215.9 %copy-start = (bf16[1,2,8,128,512]{4,3,2,1,0:T(8,128)(2,1)S(1)}, bf16[1,2,8,128,512]{4,3,2,1,0:T(8,128)(2,1)}, u32[]{:S(2)}) copy-start(bf16[1,2,8,128,512]{4,3,2,1,0:T(8,128)(2,1)} %param.26) | copy-start | bytes 6291460
  8.0 0.7 copy-start.11
  8.7 19.4 %copy-start.1 = (s32[8]{0:T(128)S(1)}, s32[8]{0:T(128)}, u32[]{:S(2)}) copy-start(s32[8]{0:T(128)} %param.23) | copy-start | bytes 100
  10.2 18.5 %copy-start.2 = (s32[8]{0:T(128)S(1)}, s32[8]{0:T(128)}, u32[]{:S(2)}) copy-start(s32[8]{0:T(128)} %param.24) | copy-start | bytes 100
  11.0 15.2 %all-to-all-start = ((bf16[8,64,256]{2,1,0:T(8,128)(2,1)}), bf16[8,64,256]{2,1,0:T(8,128)(2,1)S(1)}, u32[]{:S(2)}, u32[]{:S(2)}) async-start(bf16[8,64,256]{2,1,0:T(8,128)(2,1)} %broadcast_select_fusion.1), calls=%async_computation | async-start | bytes 524288 | tf_op jit(solution)/shard_map/all_to_all | solution.py:63
  17.3 189.5 %all-reduce.3.cloned.1.call-start = ((), (), s32[]{:S(2)}) async-start(), calls=%async_computation.4 | async-start | bytes 8388608 | tf_op jit(solution)/shard_map/psum | solution.py:126
  19.3 12.0 %copy-start.12 = (s32[8]{0:T(128)S(1)}, s32[8]{0:T(128)}, u32[]{:S(2)}) copy-start(s32[8]{0:T(128)} %param.22) | copy-start | bytes 100
  26.2 0.7 copy-start.6
  27.9 3.5 %collective-permute-start = (bf16[2,256,256]{2,1,0:T(8,128)(2,1)S(1)}, bf16[2,256,256]{2,1,0:T(8,128)(2,1)}, u32[]{:S(2)}, u32[]{:S(2)}) collective-permute-start(bf16[2,256,256]{2,1,0:T(8,128)(2,1)S(1)} %bitcast.47), channel_id=1, source_target_pairs={{0,1},{1,0},{2,3},{3,2},{4,5},{5,4},{6,7},{7,6},{8,9},{9,8},{10,11... | collective-permute-start | bytes 786440 | tf_op jit(solution)/shard_map/ppermute | solution.py:73
  32.6 14.4 %collective-permute-start.1 = (bf16[2,256,512]{2,1,0:T(8,128)(2,1)S(1)}, bf16[2,256,512]{2,1,0:T(8,128)(2,1)S(1)}, u32[]{:S(2)}, u32[]{:S(2)}) collective-permute-start(bf16[2,256,512]{2,1,0:T(8,128)(2,1)S(1)} %maximum_select_fusion.4), channel_id=1, source_target_pairs={{0,2},{1,3},{2,0},{3,1},{4,6},{5,7},{6,4},{7,5},{8,10},{9,11},{10,... | collective-permute-start | bytes 1572872 | tf_op jit(solution)/shard_map/ppermute | solution.py:73
  47.3 24.8 %copy-start.14 = (bf16[2048,256]{1,0:T(8,128)(2,1)S(1)}, bf16[2048,256]{1,0:T(8,128)(2,1)}, u32[]{:S(2)}) copy-start(bf16[2048,256]{1,0:T(8,128)(2,1)} %param.28) | copy-start | bytes 3145732
  47.3 24.8 %collective-permute-start.2 = (bf16[2,256,1024]{2,1,0:T(8,128)(2,1)S(1)}, bf16[2,256,1024]{2,1,0:T(8,128)(2,1)S(1)}, u32[]{:S(2)}, u32[]{:S(2)}) collective-permute-start(bf16[2,256,1024]{2,1,0:T(8,128)(2,1)S(1)} %maximum_select_fusion.2), channel_id=1, source_target_pairs={{0,4},{1,5},{2,6},{3,7},{4,0},{5,1},{6,2},{7,3},{8,12},{9,13},{10,... | collective-permute-start | bytes 3145736 | tf_op jit(solution)/shard_map/ppermute | solution.py:73
  72.1 1.7 copy-start.7
  72.1 1.7 copy-start.15
  116.9 1.9 copy-start.5
  120.0 1.0 copy-start.8
  120.0 1.1 copy-start.9
  128.2 81.3 %copy-start.10 = (f32[2048]{0:T(1024)S(1)}, f32[2048]{0:T(1024)}, u32[]{:S(2)}) copy-start(f32[2048]{0:T(1024)} %param.33) | copy-start | bytes 24580
  128.2 146.4 %reduce-scatter.2.cloned.1.call-start = ((), (), s32[]{:S(2)}) async-start(), calls=%async_computation.5 | async-start | bytes 4718592 | tf_op jit(solution)/shard_map/reduce_scatter | solution.py:136
  206.8 3.4 %copy-start.3 = (f32[512,2048]{1,0:T(8,128)S(1)}, f32[512,2048]{1,0:T(8,128)}, u32[]{:S(2)}) copy-start(f32[512,2048]{1,0:T(8,128)} %all-reduce.3.cloned.1.call-done) | copy-start | bytes 12582916
  210.2 4.3 %copy-start.13 = (bf16[2048,512]{1,0:T(8,128)(2,1)S(1)}, bf16[2048,512]{1,0:T(8,128)(2,1)}, u32[]{:S(2)}) copy-start(bf16[2048,512]{1,0:T(8,128)(2,1)} %param.35) | copy-start | bytes 6291460
  213.2 1.3 copy-start.4
  228.3 62.8 %all-to-all-start.2 = ((bf16[1,2,8,128,512]{4,3,1,0,2:T(8,128)(2,1)}), bf16[1,2,8,128,512]{4,3,1,0,2:T(8,128)(2,1)}, u32[]{:S(2)}, u32[]{:S(2)}) async-start(bf16[1,2,8,128,512]{4,3,1,0,2:T(8,128)(2,1)} %bitcast_select_fusion), calls=%async_computation.3 | async-start | bytes 4194304 | tf_op jit(solution)/shard_map/all_to_all | solution.py:62
  291.1 12.4 %all-to-all-start.1 = ((bf16[2,256,256]{2,0,1:T(2,128)(2,1)}), bf16[2,256,256]{2,0,1:T(2,128)(2,1)S(1)}, u32[]{:S(2)}, u32[]{:S(2)}) async-start(bf16[2,256,256]{2,0,1:T(2,128)(2,1)} %copy.65), calls=%async_computation.2 | async-start | bytes 524288 | tf_op jit(solution)/shard_map/all_to_all | solution.py:29
Sparse Core Ops, SparseCore 0:
  128.4 78.3 all-reduce.2
  223.2 51.3 reduce-scatter.1
